TPU v7x, 128 devices: a whole 4x4x4 slice. The times are simulated.
128 devices in a mesh: chan: 16 (over x, y_lo, core), win: 8 (over y_hi, z).
Axes of the slice: x: 4, y: 4 (y_hi: 2, y_lo: 2; y = y_hi * 2 + y_lo), z: 4, core: 2. Of those that a mesh axis runs over, the one named last changes fastest.
Arguments:
- traces: bfloat16 [128, 1024, 512], P('win', 'chan'), may hold values from -80 to 80
- valid: int32 [128, 1024], P('win', 'chan'), may hold values 0 or 1
- reach: int32 [1024], P('chan'), may hold values from 1 to 256
Outputs:
- stack: float32 [256, 1024, 256], P('win', 'chan')
All inputs are finite; a program needn't handle non-finite values. No bound on the sum of `valid` on one device may be relied on, other than what follows from the above.
Results may differ from a plain program's by a relative error of at most 0.0045.
Values may be sent and summed in bfloat16 or wider, within the bound.
A program may use at most 128 MiB of HBM per device.

v0:
```python
import math

import jax
import jax.numpy as jnp
from jax import lax
from jax.sharding import PartitionSpec as P

F = 128
FIRST = 16
BAND = 256


def passed_along(array, axis, by):
    peers = lax.axis_size(axis)
    return lax.ppermute(array, axis, [(i, (i + by) % peers) for i in range(peers)])


def make_table(samples):
    t_int = jnp.arange(samples, dtype=jnp.int32)
    j_int = jnp.arange(F, dtype=jnp.int32) + FIRST
    phase = t_int[:, None] * j_int[None, :] % samples
    angle = 2.0 * math.pi / samples * phase.astype(jnp.float32)
    hann = 0.5 - 0.5 * jnp.cos(2.0 * math.pi / samples * t_int.astype(jnp.float32))
    return jnp.concatenate(
        [hann[:, None] * jnp.cos(angle), -hann[:, None] * jnp.sin(angle)], axis=1
    ).astype(jnp.bfloat16)


def whiten(spectra, valid):
    real_part = spectra[..., :F]
    imag_part = spectra[..., F:]
    amplitude = jnp.sqrt(real_part * real_part + imag_part * imag_part)
    level = jnp.sqrt(jnp.mean(amplitude * amplitude, axis=-1, keepdims=True) + 1e-06)
    factor = valid.astype(jnp.float32)[..., None] / (amplitude + 0.1 * level)
    return jnp.concatenate([real_part * factor, imag_part * factor], axis=-1).astype(jnp.bfloat16)


def extend(spectra, first_offset):
    width = spectra.shape[1]
    count = BAND // width
    pieces = [spectra]
    for step in range(1, count + 1):
        pieces.append(passed_along(spectra, "chan", -step))
    return (jnp.concatenate(pieces, axis=1), first_offset)


def accumulate(carry, extended, first_offset):
    width = carry.shape[1]
    offsets = carry.shape[0]
    block = math.gcd(offsets, 16)
    own = extended[:, :width]
    a_re = own[..., :F]
    a_im = own[..., F:]

    def one_block(index, total):
        begin = first_offset + index * block
        terms = []
        for shift_by in range(block):
            partner = lax.dynamic_slice_in_dim(extended, begin + shift_by, width, 1)
            b_re = partner[..., :F]
            b_im = partner[..., F:]
            real_sum = jnp.sum(
                a_re.astype(jnp.float32) * b_re.astype(jnp.float32)
                + a_im.astype(jnp.float32) * b_im.astype(jnp.float32),
                axis=0,
            )
            imag_sum = jnp.sum(
                a_im.astype(jnp.float32) * b_re.astype(jnp.float32)
                - a_re.astype(jnp.float32) * b_im.astype(jnp.float32),
                axis=0,
            )
            terms.append(jnp.concatenate([real_sum, imag_sum], axis=-1))
        term = jnp.stack(terms, axis=0)
        before = lax.dynamic_slice_in_dim(total, index * block, block, 0)
        return lax.dynamic_update_slice_in_dim(total, before + term, index * block, 0)

    return lax.fori_loop(0, offsets // block, one_block, carry)


def on_device(traces, valid, reach):
    samples = traces.shape[2]
    local_windows = traces.shape[0]
    width = traces.shape[1]
    groups = lax.axis_size("win")
    offsets = BAND // groups
    first_offset = lax.axis_index("win") * offsets
    table = make_table(samples)
    spectra = jnp.einsum("wct,tj->wcj", traces, table, preferred_element_type=jnp.float32)
    whitened = whiten(spectra, valid)
    initial = jnp.zeros((offsets, width, 2 * F), jnp.float32)
    every_window = lax.all_gather(whitened, "win", axis=0, tiled=True)
    extended, region_start = extend(every_window, first_offset)
    summed = accumulate(initial, extended, region_start)
    offset_ids = first_offset + jnp.arange(offsets, dtype=jnp.int32)
    inside = (offset_ids[:, None] < reach[None, :]).astype(jnp.float32)
    scale = 1.0 / math.sqrt(local_windows * groups)
    return summed * inside[:, :, None] * scale


def solution(mesh):
    in_specs = (P("win", "chan", None), P("win", "chan"), P("chan"))
    out_specs = P("win", "chan", None)
    return jax.shard_map(
        on_device, mesh=mesh, in_specs=in_specs, out_specs=out_specs, check_vma=False
    )
```

profile of v0, /device:TPU:6, one launch (start us, length us, event | category | flops | bytes accessed | tf_op | source)
XLA Modules:
  0.0 587.8 jit_solution(4245023378735557408)
XLA Ops:
  6.6 1.2 multiply_convert_fusion.3
  7.8 0.4 convolution_bitcast_fusion
  8.2 0.3 multiply_reduce_fusion
  8.5 0.7 convert_element_type.465
  9.2 0.4 multiply_convert_fusion.1
  9.6 0.9 pad_maximum_fusion
  10.5 73.7 %all-gather.2.cloned.1.call-done = bf16[128,64,256]{2,1,0:T(8,128)(2,1)} async-done(((bf16[16,64,256]{2,1,0:T(8,128)(2,1)}), bf16[128,64,256]{2,1,0:T(8,128)(2,1)}) %all-gather.2.cloned.1.call-update) | async-done | bytes 4194320 | tf_op jit(solution)/shard_map/all_gather | solution.py:91
  84.2 1.0 collective-permute-start.1
  85.2 0.2 collective-permute-start.2
  85.5 0.6 collective-permute-start.3
  86.0 0.1 compare_convert_fusion
  86.1 2.7 constant_dynamic-update-slice_fusion.4
  88.8 0.8 copy-done.2
  89.5 2.6 fusion.90
  92.1 82.9 %collective-permute-done = bf16[128,64,256]{2,1,0:T(8,128)(2,1)} collective-permute-done((bf16[128,64,256]{2,1,0:T(8,128)(2,1)}, bf16[128,64,256]{2,1,0:T(8,128)(2,1)}, u32[]{:S(2)}, u32[]{:S(2)}) %collective-permute-start) | collective-permute-done | bytes 4194336 | tf_op jit(solution)/shard_map/ppermute | solution.py:15
  175.1 2.5 constant_dynamic-update-slice_fusion.3
  177.6 88.2 %collective-permute-done.1 = bf16[128,64,256]{2,1,0:T(8,128)(2,1)} collective-permute-done((bf16[128,64,256]{2,1,0:T(8,128)(2,1)}, bf16[128,64,256]{2,1,0:T(8,128)(2,1)}, u32[]{:S(2)}, u32[]{:S(2)}) %collective-permute-start.1) | collective-permute-done | bytes 4194336 | tf_op jit(solution)/shard_map/ppermute | solution.py:15
  265.7 2.5 constant_dynamic-update-slice_fusion.2
  268.2 86.6 %collective-permute-done.2 = bf16[128,64,256]{2,1,0:T(8,128)(2,1)} collective-permute-done((bf16[128,64,256]{2,1,0:T(8,128)(2,1)}, bf16[128,64,256]{2,1,0:T(8,128)(2,1)}, u32[]{:S(2)}, u32[]{:S(2)}) %collective-permute-start.2) | collective-permute-done | bytes 4194336 | tf_op jit(solution)/shard_map/ppermute | solution.py:15
  354.8 2.5 constant_dynamic-update-slice_fusion.1
  357.3 45.3 %collective-permute-done.3 = bf16[128,64,256]{2,1,0:T(8,128)(2,1)} collective-permute-done((bf16[128,64,256]{2,1,0:T(8,128)(2,1)}, bf16[128,64,256]{2,1,0:T(8,128)(2,1)}, u32[]{:S(2)}, u32[]{:S(2)}) %collective-permute-start.3) | collective-permute-done | bytes 4194336 | tf_op jit(solution)/shard_map/ppermute | solution.py:15
  402.6 2.5 constant_dynamic-update-slice_fusion
  405.1 1.8 broadcast_in_dim.2
  406.9 5.8 copy-done.1
  412.7 165.0 %while.15 = (s32[]{:T(128)}, f32[32,64,256]{2,1,0:T(8,128)}, bf16[128,64,128]{2,1,0:T(8,128)(2,1)}, s32[]{:T(128)}, bf16[128,320,256]{2,1,0:T(8,128)(2,1)}, /*in...) while((s32[]{:T(128)}, f32[32,64,256]{2,1,0:T(8,128)}, ...), condition=%wide.region_34.35_spmd, body=%wide.region_1.34_spmd.sunk | while | flops 172228672 | bytes 81790144 | solution.py:77
  412.7 62.9 %fusion.110 = (f32[64,128]{1,0:T(8,128)S(1)}, f32[64,128]{1,0:T(8,128)S(1)}, f32[64,128]{1,0:T(8,128)S(1)}, f32[64,128]{1,0:T(8,128)S(1)}, f32[64,128]{1,0:T(8,1...) fusion(bf16[128,64,128]{2,1,0:T(8,128)(2,1)} %get-tuple-element, ...), kind=kLoop, calls=%fused_computation.125.clone.1 | loop fusion | flops 159137792 | bytes 68091968 | tf_op jit(solution)/shard_map/while/body/eval_jaxpr/reduce_sum | solution.py:62
  475.6 0.6 fusion.111
  476.3 0.6 fusion.112
  476.9 0.6 fusion.113
  477.5 0.6 fusion.114
  478.1 0.6 fusion.115
  478.8 0.6 fusion.116
  479.4 0.6 fusion.117
  480.0 0.6 fusion.118
  480.6 0.6 fusion.119
  481.2 0.6 fusion.120
  481.9 0.6 fusion.121
  482.5 0.6 fusion.122
  483.1 0.6 fusion.123
  483.7 0.6 fusion.124
  484.3 6.4 %fusion.125 = (f32[64,128]{1,0:T(8,128)S(1)}, f32[64,128]{1,0:T(8,128)S(1)}) fusion(bf16[128,64,128]{2,1,0:T(8,128)(2,1)} %get-tuple-element.411, bf16[128,64,128]{2,1,0:T(8,128)(2,1)S(1)} %get-tuple-element.414, bf16[128,320,256]{2,1,0:T(8,128)(2,1)} %get-tuple-element.413, s32[]{:T(128)S(6)} %select_n.223, s32[]{:T(128)S(6)} %add.816), kind=kLoop, calls=%fused_computation.121.clone.1 | loop fusion | flops 12566528 | bytes 8454152 | tf_op jit(solution)/shard_map/while/body/eval_jaxpr/reduce_sum | solution.py:62
  490.8 0.6 fusion.126
  491.4 0.6 fusion.127
  492.0 2.7 add_dynamic-update-slice_fusion.2
  494.7 64.0 %fusion.110 = (f32[64,128]{1,0:T(8,128)S(1)}, f32[64,128]{1,0:T(8,128)S(1)}, f32[64,128]{1,0:T(8,128)S(1)}, f32[64,128]{1,0:T(8,128)S(1)}, f32[64,128]{1,0:T(8,1...) fusion(bf16[128,64,128]{2,1,0:T(8,128)(2,1)} %get-tuple-element, ...), kind=kLoop, calls=%fused_computation.125.clone.1 | loop fusion | flops 159137792 | bytes 68091968 | tf_op jit(solution)/shard_map/while/body/eval_jaxpr/reduce_sum | solution.py:62
  558.7 0.6 fusion.111
  559.3 0.6 fusion.112
  559.9 0.6 fusion.113
  560.6 0.6 fusion.114
  561.2 0.6 fusion.115
  561.8 0.6 fusion.116
  562.4 0.6 fusion.117
  563.0 0.6 fusion.118
  563.7 0.6 fusion.119
  564.3 0.6 fusion.120
  564.9 0.6 fusion.121
  565.5 0.6 fusion.122
  566.2 0.6 fusion.123
  566.8 0.6 fusion.124
  567.4 6.4 %fusion.125 = (f32[64,128]{1,0:T(8,128)S(1)}, f32[64,128]{1,0:T(8,128)S(1)}) fusion(bf16[128,64,128]{2,1,0:T(8,128)(2,1)} %get-tuple-element.411, bf16[128,64,128]{2,1,0:T(8,128)(2,1)S(1)} %get-tuple-element.414, bf16[128,320,256]{2,1,0:T(8,128)(2,1)} %get-tuple-element.413, s32[]{:T(128)S(6)} %select_n.223, s32[]{:T(128)S(6)} %add.816), kind=kLoop, calls=%fused_computation.121.clone.1 | loop fusion | flops 12566528 | bytes 8454152 | tf_op jit(solution)/shard_map/while/body/eval_jaxpr/reduce_sum | solution.py:62
  573.8 0.6 fusion.126
  574.4 0.6 fusion.127
  575.1 2.7 add_dynamic-update-slice_fusion.2
  577.7 3.2 multiply_multiply_fusion
  (13 shorter events, 0.1 us)
Async XLA Ops:
  6.5 1.2 copy-start
  6.5 79.5 %copy-start.3 = (s32[64]{0:T(128)S(1)}, s32[64]{0:T(128)}, u32[]{:S(2)}) copy-start(s32[64]{0:T(128)} %param.7) | copy-start | bytes 772
  6.5 77.7 %all-gather.2.cloned.1.call-start = ((), (), s32[]{:S(2)}) async-start(), calls=%async_computation | async-start | bytes 4718592 | tf_op jit(solution)/shard_map/all_gather | solution.py:91
  84.2 90.9 %collective-permute-start = (bf16[128,64,256]{2,1,0:T(8,128)(2,1)}, bf16[128,64,256]{2,1,0:T(8,128)(2,1)}, u32[]{:S(2)}, u32[]{:S(2)}) collective-permute-start(bf16[128,64,256]{2,1,0:T(8,128)(2,1)} %all-gather.2.cloned.1.call-done), channel_id=1, source_target_pairs={{0,120},{8,0},{16,8},{24,16},{32,24},{40,32},{48,40},{56,48},{64,5... | collective-permute-start | bytes 12582920 | tf_op jit(solution)/shard_map/ppermute | solution.py:15
  84.2 181.5 %collective-permute-start.1 = (bf16[128,64,256]{2,1,0:T(8,128)(2,1)}, bf16[128,64,256]{2,1,0:T(8,128)(2,1)}, u32[]{:S(2)}, u32[]{:S(2)}) collective-permute-start(bf16[128,64,256]{2,1,0:T(8,128)(2,1)} %all-gather.2.cloned.1.call-done), channel_id=1, source_target_pairs={{0,112},{8,120},{16,0},{24,8},{32,16},{40,24},{48,32},{56,40},{64,... | collective-permute-start | bytes 12582920 | tf_op jit(solution)/shard_map/ppermute | solution.py:15
  85.2 269.6 %collective-permute-start.2 = (bf16[128,64,256]{2,1,0:T(8,128)(2,1)}, bf16[128,64,256]{2,1,0:T(8,128)(2,1)}, u32[]{:S(2)}, u32[]{:S(2)}) collective-permute-start(bf16[128,64,256]{2,1,0:T(8,128)(2,1)} %all-gather.2.cloned.1.call-done), channel_id=1, source_target_pairs={{0,104},{8,112},{16,120},{24,0},{32,8},{40,16},{48,24},{56,32},{64... | collective-permute-start | bytes 12582920 | tf_op jit(solution)/shard_map/ppermute | solution.py:15
  85.5 317.2 %collective-permute-start.3 = (bf16[128,64,256]{2,1,0:T(8,128)(2,1)}, bf16[128,64,256]{2,1,0:T(8,128)(2,1)}, u32[]{:S(2)}, u32[]{:S(2)}) collective-permute-start(bf16[128,64,256]{2,1,0:T(8,128)(2,1)} %all-gather.2.cloned.1.call-done), channel_id=1, source_target_pairs={{0,96},{8,104},{16,112},{24,120},{32,0},{40,8},{48,16},{56,24},{64... | collective-permute-start | bytes 12582920 | tf_op jit(solution)/shard_map/ppermute | solution.py:15
  86.1 3.5 copy-start.2
  405.1 7.6 %copy-start.1 = (bf16[128,320,256]{2,1,0:T(8,128)(2,1)}, bf16[128,320,256]{2,1,0:T(8,128)(2,1)S(1)}, u32[]{:S(2)}) copy-start(bf16[128,320,256]{2,1,0:T(8,128)(2,1)S(1)} %constant_dynamic-update-slice_fusion) | copy-start | bytes 62914564
Sparse Core Ops, SparseCore 0:
  10.6 73.5 all-gather.1
where the time goes:
time: 588 us
  waiting for transfers between devices  377 us (64%)
  other arithmetic  172 us (29%)
  local copies, waits for them, and re-layouts  23.6 us (4%)
  between operations  13.5 us (2%)
    ppermute x4, waiting for transfers between devices, passed_along(): lax.ppermute(array, axis, [(i, (i + by) % peers) for i in range(peers)])  303 us
    reduce_sum x4, other arithmetic, one_block(): jnp.sum(a_re.astype(jnp.float32) * b_re.astype(jnp.float32) + a_im.astype...  140 us
    all_gather x1, waiting for transfers between devices, on_device(): every_window = lax.all_gather(whitened, 'win', axis=0, tiled=True)  73.7 us
    while x30, other arithmetic  18.6 us
    unnamed x12, local copies, waits for them, and re-layouts  16.7 us
  transfers between devices with their start and end apart: 5, of which 5 were waited for; matrix products, arithmetic and copies ran while one was open for 2% of the time, Pallas kernels for 0%

commit v1 on v0

v1 whole, which is shorter than its diff:
```python
import functools
import math

import jax
import jax.numpy as jnp
import numpy as np
from jax import lax
from jax.experimental import pallas as pl
from jax.experimental.pallas import tpu as pltpu
from jax.sharding import PartitionSpec as P

F = 128
FIRST = 16
BAND = 256
LANES = 128
MESH = pl.DeviceIdType.MESH


def table_rows(samples):
    t_int = np.arange(samples, dtype=np.int64)
    j_int = np.arange(F, dtype=np.int64) + FIRST
    angle = 2.0 * np.pi / samples * (j_int[:, None] * t_int[None, :] % samples)
    hann = 0.5 - 0.5 * np.cos(2.0 * np.pi / samples * t_int)
    rows = np.concatenate([hann * np.cos(angle), -hann * np.sin(angle)], axis=0)
    return rows.astype(np.float32).astype(jnp.bfloat16)


def exchange_kernel(
    groups, near, table_ref, traces_ref, valid_ref, out_ref,
    spread, mine, every, rows, cols, stack,
    send_in, recv_in, send_halo, recv_halo, send_out, recv_out, local_sem,
):
    chan = lax.axis_index("chan")
    win = lax.axis_index("win")
    ring = lax.axis_size("chan")
    lane_of = chan % near
    base = chan - lane_of
    team = near * groups
    bins = F // team
    me = lane_of * groups + win
    width = traces_ref.shape[1]
    local = traces_ref.shape[0]
    ahead = lax.rem(chan + near, ring)
    behind = lax.rem(chan + ring - near, ring)

    def device_of(t):
        return {"chan": base + t // groups, "win": lax.rem(t, groups)}

    barrier = pltpu.get_barrier_semaphore()

    def greet(step, carry):
        pl.semaphore_signal(
            barrier, inc=1, device_id=device_of(lax.rem(me + step, team)), device_id_type=MESH
        )
        return carry

    lax.fori_loop(1, team, greet, 0)
    for other in (ahead, behind):
        pl.semaphore_signal(
            barrier, inc=1, device_id={"chan": other, "win": win}, device_id_type=MESH
        )

    lane = lax.broadcasted_iota(jnp.int32, (1, LANES), 1)
    first_half = lane < width
    valid_twice = jnp.concatenate([valid_ref[...], valid_ref[...]], axis=1).astype(jnp.float32)
    table = table_ref[...]
    for pair in range(local // 2):
        samples = traces_ref[2 * pair : 2 * pair + 2].reshape(2 * width, traces_ref.shape[2])
        spectra = lax.dot_general(
            table, samples, (((1,), (1,)), ((), ())), preferred_element_type=jnp.float32
        )
        re = spectra[:F]
        im = spectra[F:]
        power = re * re + im * im
        amplitude = jnp.sqrt(power)
        level = jnp.sqrt(jnp.mean(power, axis=0, keepdims=True) + 1e-06)
        usable = jnp.where(
            first_half, valid_twice[2 * pair : 2 * pair + 1], valid_twice[2 * pair + 1 : 2 * pair + 2]
        )
        factor = usable / (amplitude + 0.1 * level)
        re = re * factor
        im = im * factor
        spread[2 * pair * F : (2 * pair + 1) * F, :] = jnp.where(
            first_half, re, pltpu.roll(im, width, 1)
        )
        spread[(2 * pair + 1) * F : (2 * pair + 2) * F, :] = jnp.where(
            first_half, pltpu.roll(re, width, 1), im
        )

    def gather_bin(index, carry):
        mine[index] = spread[pl.ds(index, local, stride=F), :].astype(jnp.bfloat16)
        return carry

    lax.fori_loop(0, F, gather_bin, 0, unroll=8)

    pl.semaphore_wait(barrier, team + 1)

    def send_bins(step, carry):
        t = lax.rem(me + step, team)
        pltpu.make_async_remote_copy(
            src_ref=mine.at[pl.ds(t * bins, bins)],
            dst_ref=every.at[me],
            send_sem=send_in,
            recv_sem=recv_in,
            device_id=device_of(t),
            device_id_type=MESH,
        ).start()
        return carry

    lax.fori_loop(1, team, send_bins, 0)
    every[me] = mine[pl.ds(me * bins, bins)]
    arrived = every.at[pl.ds(0, team - 1)]
    pltpu.make_async_copy(arrived, arrived, recv_in).wait()

    own = near * width
    for b in range(bins):
        for a in range(near):
            block = every[groups * a : groups * (a + 1), b].reshape(groups * local, LANES)
            wide = block.astype(jnp.float32)
            turned = wide.T.astype(jnp.bfloat16)
            rows[b, width * a : width * (a + 1), :F] = turned[:width]
            rows[b, width * a : width * (a + 1), F:] = turned[width:]
            swapped = pltpu.roll(wide, width, 1)
            cols[b, a, :F] = block
            cols[b, a, F:] = jnp.where(first_half, swapped, -swapped).astype(jnp.bfloat16)
        pltpu.make_async_remote_copy(
            src_ref=rows.at[b, pl.ds(0, own)],
            dst_ref=rows.at[b, pl.ds(own, own)],
            send_sem=send_halo.at[b],
            recv_sem=recv_halo.at[b],
            device_id={"chan": behind, "win": win},
            device_id_type=MESH,
        ).start()

    shift = lax.rem(lax.broadcasted_iota(jnp.int32, (1, LANES), 1), width)
    band = BAND // groups
    for b in range(bins):
        halo = rows.at[b, pl.ds(own, own)]
        pltpu.make_async_copy(halo, halo, recv_halo.at[b]).wait()
        for a in range(near):
            product = jnp.dot(
                rows[b, width * a : width * a + width + BAND],
                cols[b, a],
                preferred_element_type=jnp.float32,
            )
            by = width // 2
            while by >= 8:
                product = jnp.where((shift & by) != 0, product[by:], product[:-by])
                by //= 2
            size = product.shape[0]
            while by >= 1:
                product = jnp.where((shift & by) != 0, pltpu.roll(product, size - by, 0), product)
                by //= 2
            stack[b, a] = product[:BAND].astype(jnp.bfloat16)

        def send_stack(step, carry):
            t = lax.rem(me + step, team)
            pltpu.make_async_remote_copy(
                src_ref=stack.at[b, t // groups, pl.ds(lax.rem(t, groups) * band, band)],
                dst_ref=out_ref.at[me * bins + b],
                send_sem=send_out,
                recv_sem=recv_out,
                device_id=device_of(t),
                device_id_type=MESH,
            ).start()
            return carry

        lax.fori_loop(1, team, send_stack, 0)
        pltpu.make_async_copy(
            stack.at[b, lane_of, pl.ds(win * band, band)], out_ref.at[me * bins + b], local_sem.at[b]
        ).start()

    for b in range(bins):
        pltpu.make_async_copy(
            stack.at[b, lane_of, pl.ds(win * band, band)], out_ref.at[me * bins + b], local_sem.at[b]
        ).wait()
        halo = rows.at[b, pl.ds(0, own)]
        pltpu.make_async_copy(halo, halo, send_halo.at[b]).wait()
    pltpu.make_async_copy(arrived, arrived, send_in).wait()
    landed = out_ref.at[pl.ds(0, (team - 1) * bins)]
    pltpu.make_async_copy(landed, landed, send_out).wait()
    pltpu.make_async_copy(landed, landed, recv_out).wait()


def exchange(traces, valid, groups, near):
    local, width, samples = traces.shape
    team = near * groups
    bins = F // team
    own = near * width
    bf16 = jnp.bfloat16
    return pl.pallas_call(
        functools.partial(exchange_kernel, groups, near),
        out_shape=jax.ShapeDtypeStruct((F, BAND // groups, LANES), bf16),
        in_specs=[pl.BlockSpec(memory_space=pltpu.VMEM)] * 3,
        out_specs=pl.BlockSpec(memory_space=pl.ANY),
        scratch_shapes=[
            pltpu.VMEM((local * F, LANES), jnp.float32),
            pltpu.VMEM((F, local, LANES), bf16),
            pltpu.VMEM((team, bins, local, LANES), bf16),
            pltpu.VMEM((bins, 2 * own, 2 * F), bf16),
            pltpu.VMEM((bins, near, 2 * F, LANES), bf16),
            pltpu.VMEM((bins, near, BAND, LANES), bf16),
            pltpu.SemaphoreType.DMA,
            pltpu.SemaphoreType.DMA,
            pltpu.SemaphoreType.DMA((bins,)),
            pltpu.SemaphoreType.DMA((bins,)),
            pltpu.SemaphoreType.DMA,
            pltpu.SemaphoreType.DMA,
            pltpu.SemaphoreType.DMA((bins,)),
        ],
        compiler_params=pltpu.CompilerParams(collective_id=0, has_side_effects=True),
        name="exchange",
    )(table_rows(samples), traces, valid)


def finish_kernel(scale, steps, stack_ref, reach_ref, out_ref, wide):
    offsets = out_ref.shape[0]
    width = out_ref.shape[1]
    wide[...] = stack_ref[...].astype(jnp.float32).reshape(F * offsets, LANES)
    reach = jnp.concatenate([reach_ref[...], reach_ref[...]], axis=1)
    first = (lax.axis_index("win") * steps + pl.program_id(0)) * offsets

    def one(k, carry):
        piece = wide[pl.ds(k, F, stride=offsets), :]
        turned = (piece * jnp.where(first + k < reach, scale, 0.0)).T
        out_ref[k, :, :F] = turned[:width]
        out_ref[k, :, F:] = turned[width:]
        return carry

    lax.fori_loop(0, offsets, one, 0, unroll=2)


def finish(stacked, reach, windows):
    band = stacked.shape[1]
    width = reach.shape[0]
    steps = 2
    offsets = band // steps
    return pl.pallas_call(
        functools.partial(finish_kernel, 1.0 / math.sqrt(windows), steps),
        out_shape=jax.ShapeDtypeStruct((band, width, 2 * F), jnp.float32),
        grid=(steps,),
        in_specs=[
            pl.BlockSpec((F, offsets, LANES), lambda s: (0, s, 0)),
            pl.BlockSpec((1, width), lambda s: (0, 0)),
        ],
        out_specs=pl.BlockSpec((offsets, width, 2 * F), lambda s: (s, 0, 0)),
        scratch_shapes=[pltpu.VMEM((F * offsets, LANES), jnp.float32)],
        name="finish",
    )(stacked, reach.reshape(1, width))


def on_device(groups, near, traces, valid, reach):
    stacked = exchange(traces, valid, groups, near)
    return finish(stacked, reach, traces.shape[0] * groups)


def solution(mesh):
    groups = mesh.shape["win"]
    near = BAND // (1024 // mesh.shape["chan"])
    in_specs = (P("win", "chan", None), P("win", "chan"), P("chan"))
    return jax.shard_map(
        functools.partial(on_device, groups, near),
        mesh=mesh,
        in_specs=in_specs,
        out_specs=P("win", "chan", None),
        check_vma=False,
    )
```

time: 588 us -> 42.8 us (0.07)
  the two profiles are of different devices: /device:TPU:6 before, /device:TPU:1 now
where the time goes in v1:
time: 42.8 us; the launch traced here: 42.6 us
  Pallas kernels  42.6 us (100%)
    pallas_call x1, Pallas kernels, exchange(): pl.pallas_call(functools.partial(exchange_kernel, groups, near), out_shap...  38.6 us
    pallas_call x1, Pallas kernels, finish(): pl.pallas_call(functools.partial(finish_kernel, 1.0 / math.sqrt(windows),...  3.97 us

profile of v1, /device:TPU:1, one launch (start us, length us, event | category | flops | bytes accessed | tf_op | source)
XLA Modules:
  0.0 42.6 jit_solution(3520057664228863765)
XLA Ops:
  0.0 38.6 %exchange.1.stack_ref = bf16[128,32,128]{2,1,0:T(8,128)(2,1)} custom-call(bf16[256,512]{1,0:T(8,128)(2,1)} %constant.2.clone.table_ref, bf16[16,64,512]{2,1,0:T(8,128)(2,1)} %traces_ref.1, s32[16,64]{1,0:T(8,128)} %valid_ref.1), custom_call_target="tpu_custom_call" | custom-call | tf_op jit(solution)/shard_map/exchange/pallas_call | solution.py:191
  38.6 4.0 %finish.1 = f32[32,64,256]{2,1,0:T(8,128)} custom-call(bf16[128,32,128]{2,1,0:T(8,128)(2,1)} %exchange.1.stack_ref, s32[1,64]{1,0:T(1,128)} %bitcast.1), custom_call_target="tpu_custom_call" | custom-call | tf_op jit(solution)/shard_map/finish/pallas_call | solution.py:238

commit v2 on v1

--- a/solution.py
+++ b/solution.py
@@ -33,7 +33,9 @@
     chan = lax.axis_index("chan")
     win = lax.axis_index("win")
     ring = lax.axis_size("chan")
-    lane_of = chan % near
+    depth = groups // 2
+    cores = near // 2
+    lane_of = lax.rem(chan, near)
     base = chan - lane_of
     team = near * groups
     bins = F // team
@@ -43,18 +45,37 @@
     ahead = lax.rem(chan + near, ring)
     behind = lax.rem(chan + ring - near, ring)
 
-    def device_of(t):
-        return {"chan": base + t // groups, "win": lax.rem(t, groups)}
+    y_hi, z = win // depth, lax.rem(win, depth)
+    y_lo, core = lane_of // cores, lax.rem(lane_of, cores)
+
+    def hops(step):
+        d_hi, d_lo, d_z, d_core = step
+        return (1 if d_lo else 2 * d_hi) + min(d_z, depth - d_z)
+
+    steps = [
+        (d_hi, d_lo, d_z, d_core)
+        for d_hi in range(2)
+        for d_lo in range(2)
+        for d_z in range(depth)
+        for d_core in range(cores)
+    ]
+    steps.sort(key=lambda step: (-hops(step), step))
+    steps.remove((0, 0, 0, 0))
+
+    def win_at(d_hi, d_z):
+        return lax.rem(y_hi + d_hi, 2) * depth + lax.rem(z + d_z, depth)
+
+    def lane_at(d_lo, d_core):
+        return lax.rem(y_lo + d_lo, 2) * cores + lax.rem(core + d_core, cores)
 
     barrier = pltpu.get_barrier_semaphore()
-
-    def greet(step, carry):
+    for d_hi, d_lo, d_z, d_core in steps:
         pl.semaphore_signal(
-            barrier, inc=1, device_id=device_of(lax.rem(me + step, team)), device_id_type=MESH
-        )
-        return carry
-
-    lax.fori_loop(1, team, greet, 0)
+            barrier,
+            inc=1,
+            device_id={"chan": base + lane_at(d_lo, d_core), "win": win_at(d_hi, d_z)},
+            device_id_type=MESH,
+        )
     for other in (ahead, behind):
         pl.semaphore_signal(
             barrier, inc=1, device_id={"chan": other, "win": win}, device_id_type=MESH
@@ -87,35 +108,44 @@
             first_half, pltpu.roll(re, width, 1), im
         )
 
-    def gather_bin(index, carry):
-        mine[index] = spread[pl.ds(index, local, stride=F), :].astype(jnp.bfloat16)
+    def gather_bins(b):
+        def gather_bin(t, carry):
+            index = b * team + t
+            mine[index] = spread[pl.ds(index, local, stride=F), :].astype(jnp.bfloat16)
+            return carry
+
+        lax.fori_loop(0, team, gather_bin, 0, unroll=8)
+
+    gather_bins(0)
+    pl.semaphore_wait(barrier, team + 1)
+
+    def send_bins(b, carry):
+        for d_hi, d_lo, d_z, d_core in steps:
+            to_lane, to_win = lane_at(d_lo, d_core), win_at(d_hi, d_z)
+            pltpu.make_async_remote_copy(
+                src_ref=mine.at[b * team + to_lane * groups + to_win],
+                dst_ref=every.at[b, me],
+                send_sem=send_in,
+                recv_sem=recv_in.at[b],
+                device_id={"chan": base + to_lane, "win": to_win},
+                device_id_type=MESH,
+            ).start()
+        every[b, me] = mine[b * team + me]
+
+        @pl.when(b + 1 < bins)
+        def _():
+            gather_bins(b + 1)
+
         return carry
 
-    lax.fori_loop(0, F, gather_bin, 0, unroll=8)
-
-    pl.semaphore_wait(barrier, team + 1)
-
-    def send_bins(step, carry):
-        t = lax.rem(me + step, team)
-        pltpu.make_async_remote_copy(
-            src_ref=mine.at[pl.ds(t * bins, bins)],
-            dst_ref=every.at[me],
-            send_sem=send_in,
-            recv_sem=recv_in,
-            device_id=device_of(t),
-            device_id_type=MESH,
-        ).start()
-        return carry
-
-    lax.fori_loop(1, team, send_bins, 0)
-    every[me] = mine[pl.ds(me * bins, bins)]
-    arrived = every.at[pl.ds(0, team - 1)]
-    pltpu.make_async_copy(arrived, arrived, recv_in).wait()
+    lax.fori_loop(0, bins, send_bins, 0)
 
     own = near * width
     for b in range(bins):
+        arrived = every.at[b, pl.ds(0, team - 1)]
+        pltpu.make_async_copy(arrived, arrived, recv_in.at[b]).wait()
         for a in range(near):
-            block = every[groups * a : groups * (a + 1), b].reshape(groups * local, LANES)
+            block = every[b, groups * a : groups * (a + 1)].reshape(groups * local, LANES)
             wide = block.astype(jnp.float32)
             turned = wide.T.astype(jnp.bfloat16)
             rows[b, width * a : width * (a + 1), :F] = turned[:width]
@@ -123,21 +153,23 @@
             swapped = pltpu.roll(wide, width, 1)
             cols[b, a, :F] = block
             cols[b, a, F:] = jnp.where(first_half, swapped, -swapped).astype(jnp.bfloat16)
-        pltpu.make_async_remote_copy(
-            src_ref=rows.at[b, pl.ds(0, own)],
-            dst_ref=rows.at[b, pl.ds(own, own)],
-            send_sem=send_halo.at[b],
-            recv_sem=recv_halo.at[b],
-            device_id={"chan": behind, "win": win},
-            device_id_type=MESH,
-        ).start()
+        for a in range(near):
+            pltpu.make_async_remote_copy(
+                src_ref=rows.at[b, pl.ds(width * a, width)],
+                dst_ref=rows.at[b, pl.ds(own + width * a, width)],
+                send_sem=send_halo,
+                recv_sem=recv_halo.at[b * near + a],
+                device_id={"chan": behind, "win": win},
+                device_id_type=MESH,
+            ).start()
 
     shift = lax.rem(lax.broadcasted_iota(jnp.int32, (1, LANES), 1), width)
     band = BAND // groups
+    order = sorted({(step[0], step[2]) for step in steps}, key=lambda s: -hops((s[0], 0, s[1], 0)))
     for b in range(bins):
-        halo = rows.at[b, pl.ds(own, own)]
-        pltpu.make_async_copy(halo, halo, recv_halo.at[b]).wait()
         for a in range(near):
+            halo = rows.at[b, pl.ds(own + width * a, width)]
+            pltpu.make_async_copy(halo, halo, recv_halo.at[b * near + a]).wait()
             product = jnp.dot(
                 rows[b, width * a : width * a + width + BAND],
                 cols[b, a],
@@ -153,30 +185,36 @@
                 by //= 2
             stack[b, a] = product[:BAND].astype(jnp.bfloat16)
 
-        def send_stack(step, carry):
-            t = lax.rem(me + step, team)
-            pltpu.make_async_remote_copy(
-                src_ref=stack.at[b, t // groups, pl.ds(lax.rem(t, groups) * band, band)],
-                dst_ref=out_ref.at[me * bins + b],
-                send_sem=send_out,
-                recv_sem=recv_out,
-                device_id=device_of(t),
-                device_id_type=MESH,
-            ).start()
-            return carry
-
-        lax.fori_loop(1, team, send_stack, 0)
-        pltpu.make_async_copy(
-            stack.at[b, lane_of, pl.ds(win * band, band)], out_ref.at[me * bins + b], local_sem.at[b]
-        ).start()
-
-    for b in range(bins):
-        pltpu.make_async_copy(
-            stack.at[b, lane_of, pl.ds(win * band, band)], out_ref.at[me * bins + b], local_sem.at[b]
-        ).wait()
-        halo = rows.at[b, pl.ds(0, own)]
-        pltpu.make_async_copy(halo, halo, send_halo.at[b]).wait()
-    pltpu.make_async_copy(arrived, arrived, send_in).wait()
+            def send_stack(d_hi, d_z, b=b, a=a):
+                to_win = win_at(d_hi, d_z)
+                pltpu.make_async_remote_copy(
+                    src_ref=stack.at[b, a, pl.ds(to_win * band, band)],
+                    dst_ref=out_ref.at[b * team + me],
+                    send_sem=send_out,
+                    recv_sem=recv_out,
+                    device_id={"chan": base + a, "win": to_win},
+                    device_id_type=MESH,
+                ).start()
+
+            for d_hi, d_z in order[:-1]:
+                send_stack(d_hi, d_z)
+
+            @pl.when(lane_of != a)
+            def _(b=b, a=a):
+                send_stack(0, 0)
+
+            @pl.when(lane_of == a)
+            def _(b=b, a=a):
+                pltpu.make_async_copy(
+                    stack.at[b, a, pl.ds(win * band, band)], out_ref.at[b * team + me], local_sem
+                ).start()
+
+    sent = mine.at[pl.ds(0, bins * (team - 1))]
+    pltpu.make_async_copy(sent, sent, send_in).wait()
+    halo = rows.at[pl.ds(0, bins), pl.ds(0, own)]
+    pltpu.make_async_copy(halo, halo, send_halo).wait()
+    here = out_ref.at[pl.ds(0, bins)]
+    pltpu.make_async_copy(here, here, local_sem).wait()
     landed = out_ref.at[pl.ds(0, (team - 1) * bins)]
     pltpu.make_async_copy(landed, landed, send_out).wait()
     pltpu.make_async_copy(landed, landed, recv_out).wait()
@@ -196,17 +234,17 @@
         scratch_shapes=[
             pltpu.VMEM((local * F, LANES), jnp.float32),
             pltpu.VMEM((F, local, LANES), bf16),
-            pltpu.VMEM((team, bins, local, LANES), bf16),
+            pltpu.VMEM((bins, team, local, LANES), bf16),
             pltpu.VMEM((bins, 2 * own, 2 * F), bf16),
             pltpu.VMEM((bins, near, 2 * F, LANES), bf16),
             pltpu.VMEM((bins, near, BAND, LANES), bf16),
             pltpu.SemaphoreType.DMA,
-            pltpu.SemaphoreType.DMA,
             pltpu.SemaphoreType.DMA((bins,)),
-            pltpu.SemaphoreType.DMA((bins,)),
-            pltpu.SemaphoreType.DMA,
-            pltpu.SemaphoreType.DMA,
-            pltpu.SemaphoreType.DMA((bins,)),
+            pltpu.SemaphoreType.DMA,
+            pltpu.SemaphoreType.DMA((bins * near,)),
+            pltpu.SemaphoreType.DMA,
+            pltpu.SemaphoreType.DMA,
+            pltpu.SemaphoreType.DMA,
         ],
         compiler_params=pltpu.CompilerParams(collective_id=0, has_side_effects=True),
         name="exchange",

time: 42.8 us -> 37.3 us (0.87)
  Pallas kernels: 42.6 us -> 37.2 us
    pallas_call x1, Pallas kernels: 38.6 us -> 33.2 us  [exchange(): pl.pallas_call(functools.partial(exchange_kernel, groups, near), out_shap...]
where the time goes in v2:
time: 37.3 us; the launch traced here: 37.2 us
  Pallas kernels  37.2 us (100%)
    pallas_call x1, Pallas kernels, exchange(): pl.pallas_call(functools.partial(exchange_kernel, groups, near), out_shap...  33.2 us
    pallas_call x1, Pallas kernels, finish(): pl.pallas_call(functools.partial(finish_kernel, 1.0 / math.sqrt(windows),...  3.97 us

profile of v2, /device:TPU:1, one launch (start us, length us, event | category | flops | bytes accessed | tf_op | source)
XLA Modules:
  0.0 37.2 jit_solution(12423663610727502744)
XLA Ops:
  0.0 33.2 %exchange.1.stack_ref = bf16[128,32,128]{2,1,0:T(8,128)(2,1)} custom-call(bf16[256,512]{1,0:T(8,128)(2,1)} %constant.2.clone.table_ref, bf16[16,64,512]{2,1,0:T(8,128)(2,1)} %traces_ref.1, s32[16,64]{1,0:T(8,128)} %valid_ref.1), custom_call_target="tpu_custom_call" | custom-call | tf_op jit(solution)/shard_map/exchange/pallas_call | solution.py:229
  33.2 4.0 %finish.1 = f32[32,64,256]{2,1,0:T(8,128)} custom-call(bf16[128,32,128]{2,1,0:T(8,128)(2,1)} %exchange.1.stack_ref, s32[1,64]{1,0:T(1,128)} %bitcast.1), custom_call_target="tpu_custom_call" | custom-call | tf_op jit(solution)/shard_map/finish/pallas_call | solution.py:276

commit v3 on v2

--- a/solution.py
+++ b/solution.py
@@ -26,9 +26,9 @@
 
 
 def exchange_kernel(
-    groups, near, table_ref, traces_ref, valid_ref, out_ref,
-    spread, mine, every, rows, cols, stack,
-    send_in, recv_in, send_halo, recv_halo, send_out, recv_out, local_sem,
+    groups, near, scale, table_hbm, traces_hbm, valid_hbm, reach_hbm, out_ref, weight_ref,
+    table_ref, traces_ref, valid_ref, reach_ref, spread, mine, every, rows, cols, stack, landing, wide,
+    load_sem, send_in, recv_in, send_halo, recv_halo, send_out, recv_out,
 ):
     chan = lax.axis_index("chan")
     win = lax.axis_index("win")
@@ -68,6 +68,15 @@
     def lane_at(d_lo, d_core):
         return lax.rem(y_lo + d_lo, 2) * cores + lax.rem(core + d_core, cores)
 
+    loads = [
+        pltpu.make_async_copy(table_hbm, table_ref, load_sem.at[0]),
+        pltpu.make_async_copy(traces_hbm, traces_ref, load_sem.at[1]),
+        pltpu.make_async_copy(valid_hbm, valid_ref, load_sem.at[2]),
+        pltpu.make_async_copy(reach_hbm, reach_ref, load_sem.at[3]),
+    ]
+    for load in loads:
+        load.start()
+
     barrier = pltpu.get_barrier_semaphore()
     for d_hi, d_lo, d_z, d_core in steps:
         pl.semaphore_signal(
@@ -81,14 +90,16 @@
             barrier, inc=1, device_id={"chan": other, "win": win}, device_id_type=MESH
         )
 
+    for load in loads:
+        load.wait()
+
     lane = lax.broadcasted_iota(jnp.int32, (1, LANES), 1)
     first_half = lane < width
     valid_twice = jnp.concatenate([valid_ref[...], valid_ref[...]], axis=1).astype(jnp.float32)
-    table = table_ref[...]
     for pair in range(local // 2):
         samples = traces_ref[2 * pair : 2 * pair + 2].reshape(2 * width, traces_ref.shape[2])
         spectra = lax.dot_general(
-            table, samples, (((1,), (1,)), ((), ())), preferred_element_type=jnp.float32
+            table_ref[...], samples, (((1,), (1,)), ((), ())), preferred_element_type=jnp.float32
         )
         re = spectra[:F]
         im = spectra[F:]
@@ -101,22 +112,18 @@
         factor = usable / (amplitude + 0.1 * level)
         re = re * factor
         im = im * factor
-        spread[2 * pair * F : (2 * pair + 1) * F, :] = jnp.where(
+        spread[2 * pair * F : 2 * pair * F + F, :] = jnp.where(
             first_half, re, pltpu.roll(im, width, 1)
         )
-        spread[(2 * pair + 1) * F : (2 * pair + 2) * F, :] = jnp.where(
+        spread[(2 * pair + 1) * F : (2 * pair + 1) * F + F, :] = jnp.where(
             first_half, pltpu.roll(re, width, 1), im
         )
 
-    def gather_bins(b):
-        def gather_bin(t, carry):
-            index = b * team + t
-            mine[index] = spread[pl.ds(index, local, stride=F), :].astype(jnp.bfloat16)
-            return carry
-
-        lax.fori_loop(0, team, gather_bin, 0, unroll=8)
-
-    gather_bins(0)
+    def gather_bin(index, carry):
+        mine[index] = spread[pl.ds(index, local, stride=F), :].astype(jnp.bfloat16)
+        return carry
+
+    lax.fori_loop(0, F, gather_bin, 0, unroll=8)
     pl.semaphore_wait(barrier, team + 1)
 
     def send_bins(b, carry):
@@ -131,17 +138,13 @@
                 device_id_type=MESH,
             ).start()
         every[b, me] = mine[b * team + me]
-
-        @pl.when(b + 1 < bins)
-        def _():
-            gather_bins(b + 1)
-
         return carry
 
     lax.fori_loop(0, bins, send_bins, 0)
 
     own = near * width
-    for b in range(bins):
+
+    def turn(b):
         arrived = every.at[b, pl.ds(0, team - 1)]
         pltpu.make_async_copy(arrived, arrived, recv_in.at[b]).wait()
         for a in range(near):
@@ -166,7 +169,8 @@
     shift = lax.rem(lax.broadcasted_iota(jnp.int32, (1, LANES), 1), width)
     band = BAND // groups
     order = sorted({(step[0], step[2]) for step in steps}, key=lambda s: -hops((s[0], 0, s[1], 0)))
-    for b in range(bins):
+
+    def multiply(b):
         for a in range(near):
             halo = rows.at[b, pl.ds(own + width * a, width)]
             pltpu.make_async_copy(halo, halo, recv_halo.at[b * near + a]).wait()
@@ -189,9 +193,9 @@
                 to_win = win_at(d_hi, d_z)
                 pltpu.make_async_remote_copy(
                     src_ref=stack.at[b, a, pl.ds(to_win * band, band)],
-                    dst_ref=out_ref.at[b * team + me],
+                    dst_ref=landing.at[b * team + me],
                     send_sem=send_out,
-                    recv_sem=recv_out,
+                    recv_sem=recv_out.at[b],
                     device_id={"chan": base + a, "win": to_win},
                     device_id_type=MESH,
                 ).start()
@@ -205,91 +209,111 @@
 
             @pl.when(lane_of == a)
             def _(b=b, a=a):
-                pltpu.make_async_copy(
-                    stack.at[b, a, pl.ds(win * band, band)], out_ref.at[b * team + me], local_sem
-                ).start()
+                landing[b * team + me] = stack[b, a, pl.ds(pl.multiple_of(win * band, band), band)]
+
+    turn(0)
+    for b in range(1, bins):
+        turn(b)
+        multiply(b - 1)
+    multiply(bins - 1)
+
+    reach = jnp.concatenate([reach_ref[...], reach_ref[...]], axis=1)
+    offset = win * band + lax.broadcasted_iota(jnp.int32, (band, LANES), 0)
+    weight_ref[...] = jnp.where(offset < reach, scale, 0.0)
+    for b in range(bins):
+        pieces = landing.at[pl.ds(b * team, team - 1)]
+        pltpu.make_async_copy(pieces, pieces, recv_out.at[b]).wait()
+        wide[...] = (
+            landing[b * team : (b + 1) * team].astype(jnp.float32).reshape(team * band, LANES)
+        )
+        for k in range(band):
+            out_ref[k, b * team : (b + 1) * team] = wide[pl.ds(k, team, stride=band), :].astype(
+                jnp.bfloat16
+            )
 
     sent = mine.at[pl.ds(0, bins * (team - 1))]
     pltpu.make_async_copy(sent, sent, send_in).wait()
     halo = rows.at[pl.ds(0, bins), pl.ds(0, own)]
     pltpu.make_async_copy(halo, halo, send_halo).wait()
-    here = out_ref.at[pl.ds(0, bins)]
-    pltpu.make_async_copy(here, here, local_sem).wait()
-    landed = out_ref.at[pl.ds(0, (team - 1) * bins)]
+    landed = landing.at[pl.ds(0, (team - 1) * bins)]
     pltpu.make_async_copy(landed, landed, send_out).wait()
-    pltpu.make_async_copy(landed, landed, recv_out).wait()
-
-
-def exchange(traces, valid, groups, near):
+
+
+def exchange(traces, valid, reach, groups, near):
     local, width, samples = traces.shape
     team = near * groups
     bins = F // team
     own = near * width
+    band = BAND // groups
     bf16 = jnp.bfloat16
     return pl.pallas_call(
-        functools.partial(exchange_kernel, groups, near),
-        out_shape=jax.ShapeDtypeStruct((F, BAND // groups, LANES), bf16),
-        in_specs=[pl.BlockSpec(memory_space=pltpu.VMEM)] * 3,
-        out_specs=pl.BlockSpec(memory_space=pl.ANY),
+        functools.partial(exchange_kernel, groups, near, 1.0 / math.sqrt(local * groups)),
+        out_shape=(pltpu.VMEM((band, F, LANES), bf16), pltpu.VMEM((band, LANES), jnp.float32)),
+        in_specs=[pl.BlockSpec(memory_space=pl.ANY)] * 4,
+        out_specs=(pl.BlockSpec(memory_space=pltpu.VMEM),) * 2,
         scratch_shapes=[
+            pltpu.VMEM((2 * F, samples), bf16),
+            pltpu.VMEM((local, width, samples), bf16),
+            pltpu.VMEM((local, width), jnp.int32),
+            pltpu.VMEM((1, width), jnp.int32),
             pltpu.VMEM((local * F, LANES), jnp.float32),
             pltpu.VMEM((F, local, LANES), bf16),
             pltpu.VMEM((bins, team, local, LANES), bf16),
             pltpu.VMEM((bins, 2 * own, 2 * F), bf16),
             pltpu.VMEM((bins, near, 2 * F, LANES), bf16),
             pltpu.VMEM((bins, near, BAND, LANES), bf16),
+            pltpu.VMEM((F, band, LANES), bf16),
+            pltpu.VMEM((team * band, LANES), jnp.float32),
+            pltpu.SemaphoreType.DMA((4,)),
             pltpu.SemaphoreType.DMA,
             pltpu.SemaphoreType.DMA((bins,)),
             pltpu.SemaphoreType.DMA,
             pltpu.SemaphoreType.DMA((bins * near,)),
             pltpu.SemaphoreType.DMA,
-            pltpu.SemaphoreType.DMA,
-            pltpu.SemaphoreType.DMA,
+            pltpu.SemaphoreType.DMA((bins,)),
         ],
         compiler_params=pltpu.CompilerParams(collective_id=0, has_side_effects=True),
         name="exchange",
-    )(table_rows(samples), traces, valid)
-
-
-def finish_kernel(scale, steps, stack_ref, reach_ref, out_ref, wide):
-    offsets = out_ref.shape[0]
-    width = out_ref.shape[1]
-    wide[...] = stack_ref[...].astype(jnp.float32).reshape(F * offsets, LANES)
-    reach = jnp.concatenate([reach_ref[...], reach_ref[...]], axis=1)
-    first = (lax.axis_index("win") * steps + pl.program_id(0)) * offsets
-
-    def one(k, carry):
-        piece = wide[pl.ds(k, F, stride=offsets), :]
-        turned = (piece * jnp.where(first + k < reach, scale, 0.0)).T
-        out_ref[k, :, :F] = turned[:width]
-        out_ref[k, :, F:] = turned[width:]
-        return carry
-
-    lax.fori_loop(0, offsets, one, 0, unroll=2)
-
-
-def finish(stacked, reach, windows):
-    band = stacked.shape[1]
-    width = reach.shape[0]
-    steps = 2
-    offsets = band // steps
+    )(table_rows(samples), traces, valid, reach.reshape(1, width))
+
+
+def finish_kernel(parts, stack_ref, weight_ref, out_ref, done, sems):
+    band, width = out_ref.shape[0], out_ref.shape[1]
+    size = band // parts
+    copies = []
+    for part in range(parts):
+        for k in range(part * size, (part + 1) * size):
+            turned = (stack_ref[k].astype(jnp.float32) * weight_ref[k : k + 1]).T
+            done[k, :, :F] = turned[:width]
+            done[k, :, F:] = turned[width:]
+        piece = pl.ds(part * size, size)
+        copies.append(pltpu.make_async_copy(done.at[piece], out_ref.at[piece], sems.at[part]))
+        copies[-1].start()
+    for copy in copies:
+        copy.wait()
+
+
+def finish(stacked, weights, width):
+    band = stacked.shape[0]
+    parts = 8
+    stacked = pltpu.with_memory_space_constraint(stacked, pltpu.VMEM)
+    weights = pltpu.with_memory_space_constraint(weights, pltpu.VMEM)
     return pl.pallas_call(
-        functools.partial(finish_kernel, 1.0 / math.sqrt(windows), steps),
+        functools.partial(finish_kernel, parts),
         out_shape=jax.ShapeDtypeStruct((band, width, 2 * F), jnp.float32),
-        grid=(steps,),
-        in_specs=[
-            pl.BlockSpec((F, offsets, LANES), lambda s: (0, s, 0)),
-            pl.BlockSpec((1, width), lambda s: (0, 0)),
+        in_specs=[pl.BlockSpec(memory_space=pltpu.VMEM)] * 2,
+        out_specs=pl.BlockSpec(memory_space=pl.ANY),
+        scratch_shapes=[
+            pltpu.VMEM((band, width, 2 * F), jnp.float32),
+            pltpu.SemaphoreType.DMA((parts,)),
         ],
-        out_specs=pl.BlockSpec((offsets, width, 2 * F), lambda s: (s, 0, 0)),
-        scratch_shapes=[pltpu.VMEM((F * offsets, LANES), jnp.float32)],
         name="finish",
-    )(stacked, reach.reshape(1, width))
+    )(stacked, weights)
 
 
 def on_device(groups, near, traces, valid, reach):
-    stacked = exchange(traces, valid, groups, near)
-    return finish(stacked, reach, traces.shape[0] * groups)
+    stacked, weights = exchange(traces, valid, reach, groups, near)
+    return finish(stacked, weights, traces.shape[1])
 
 
 def solution(mesh):

time: 37.3 us -> 33.4 us (0.90)
  Pallas kernels: 37.2 us -> 33.3 us
    pallas_call x2, Pallas kernels: 37.2 us -> 33.3 us  [the longest x1 31.8 us: exchange(): pl.pallas_call(functools.partial(exchange_kernel, groups, near, 1.0 / mat...]
where the time goes in v3:
time: 33.4 us; the launch traced here: 33.3 us
  Pallas kernels  33.3 us (100%)
    pallas_call x1, Pallas kernels, exchange(): pl.pallas_call(functools.partial(exchange_kernel, groups, near, 1.0 / mat...  31.8 us
    pallas_call x1, Pallas kernels, finish(): pl.pallas_call(functools.partial(finish_kernel, parts), out_shape=jax.Sha...  1.51 us

profile of v3, /device:TPU:1, one launch (start us, length us, event | category | flops | bytes accessed | tf_op | source)
XLA Modules:
  0.0 33.3 jit_solution(17489069224386381445)
XLA Ops:
  0.0 31.8 %exchange.1 = (bf16[32,128,128]{2,1,0:T(8,128)(2,1)S(1)}, f32[32,128]{1,0:T(8,128)S(1)}) custom-call(bf16[256,512]{1,0:T(8,128)(2,1)} %constant.2.clone.table_hbm, bf16[16,64,512]{2,1,0:T(8,128)(2,1)} %traces_hbm.1, s32[16,64]{1,0:T(8,128)} %valid_hbm.1, s32[1,64]{1,0:T(1,128)} %bitcast.1), custom_call_target="tpu_custom_call" | custom-call | tf_op jit(solution)/shard_map/exchange/pallas_call | solution.py:249
  31.8 1.5 %finish.1 = f32[32,64,256]{2,1,0:T(8,128)} custom-call(bf16[32,128,128]{2,1,0:T(8,128)(2,1)S(1)} %get-tuple-element.7.stack_ref, f32[32,128]{1,0:T(8,128)S(1)} %get-tuple-element.8.weight_ref), custom_call_target="tpu_custom_call" | custom-call | tf_op jit(solution)/shard_map/finish/pallas_call | solution.py:301

commit v4 on v3

--- a/solution.py
+++ b/solution.py
@@ -170,27 +170,30 @@
     band = BAND // groups
     order = sorted({(step[0], step[2]) for step in steps}, key=lambda s: -hops((s[0], 0, s[1], 0)))
 
-    def multiply(b):
-        for a in range(near):
-            halo = rows.at[b, pl.ds(own + width * a, width)]
-            pltpu.make_async_copy(halo, halo, recv_halo.at[b * near + a]).wait()
-            product = jnp.dot(
-                rows[b, width * a : width * a + width + BAND],
-                cols[b, a],
-                preferred_element_type=jnp.float32,
-            )
-            by = width // 2
-            while by >= 8:
-                product = jnp.where((shift & by) != 0, product[by:], product[:-by])
-                by //= 2
-            size = product.shape[0]
-            while by >= 1:
-                product = jnp.where((shift & by) != 0, pltpu.roll(product, size - by, 0), product)
-                by //= 2
-            stack[b, a] = product[:BAND].astype(jnp.bfloat16)
-
-            def send_stack(d_hi, d_z, b=b, a=a):
-                to_win = win_at(d_hi, d_z)
+    def early(a):
+        return max(0, (own - width * a - width) // band)
+
+    def piece(b, a, start, stop):
+        first = width * a + band * start
+        product = jnp.dot(
+            rows[b, first : first + band * (stop - start) + width],
+            cols[b, a],
+            preferred_element_type=jnp.float32,
+        )
+        by = width // 2
+        while by >= 8:
+            product = jnp.where((shift & by) != 0, product[by:], product[:-by])
+            by //= 2
+        size = product.shape[0]
+        while by >= 1:
+            product = jnp.where((shift & by) != 0, pltpu.roll(product, size - by, 0), product)
+            by //= 2
+        stack[b, a, band * start : band * stop] = product[: band * (stop - start)].astype(jnp.bfloat16)
+
+        def send_stack(d_hi, d_z):
+            to_win = win_at(d_hi, d_z)
+
+            def send():
                 pltpu.make_async_remote_copy(
                     src_ref=stack.at[b, a, pl.ds(to_win * band, band)],
                     dst_ref=landing.at[b * team + me],
@@ -200,21 +203,40 @@
                     device_id_type=MESH,
                 ).start()
 
-            for d_hi, d_z in order[:-1]:
-                send_stack(d_hi, d_z)
-
-            @pl.when(lane_of != a)
-            def _(b=b, a=a):
-                send_stack(0, 0)
+            if start == 0 and stop == groups:
+                send()
+            else:
+                pl.when((to_win >= start) & (to_win < stop))(send)
+
+        for d_hi, d_z in order[:-1]:
+            send_stack(d_hi, d_z)
+
+        @pl.when(lane_of != a)
+        def _():
+            send_stack(0, 0)
+
+        if stop == groups:
 
             @pl.when(lane_of == a)
-            def _(b=b, a=a):
+            def _():
                 landing[b * team + me] = stack[b, a, pl.ds(pl.multiple_of(win * band, band), band)]
 
-    turn(0)
-    for b in range(1, bins):
+    def multiply_early(b):
+        for a in range(near):
+            if early(a):
+                piece(b, a, 0, early(a))
+
+    def multiply(b):
+        for a in range(near):
+            halo = rows.at[b, pl.ds(own + width * a, width)]
+            pltpu.make_async_copy(halo, halo, recv_halo.at[b * near + a]).wait()
+            piece(b, a, early(a), groups)
+
+    for b in range(bins):
         turn(b)
-        multiply(b - 1)
+        multiply_early(b)
+        if b > 0:
+            multiply(b - 1)
     multiply(bins - 1)
 
     reach = jnp.concatenate([reach_ref[...], reach_ref[...]], axis=1)

time: 33.4 us -> 32.1 us (0.961)
  the two profiles are of different devices: /device:TPU:1 before, /device:TPU:27 now
where the time goes in v4:
time: 32.1 us; the launch traced here: 32 us
  Pallas kernels  32 us (100%)
    pallas_call x1, Pallas kernels, exchange(): pl.pallas_call(functools.partial(exchange_kernel, groups, near, 1.0 / mat...  30.5 us
    pallas_call x1, Pallas kernels, finish(): pl.pallas_call(functools.partial(finish_kernel, parts), out_shape=jax.Sha...  1.51 us

profile of v4, /device:TPU:27, one launch (start us, length us, event | category | flops | bytes accessed | tf_op | source)
XLA Modules:
  0.0 32.0 jit_solution(4430166368305332879)
XLA Ops:
  0.0 30.5 %exchange.1 = (bf16[32,128,128]{2,1,0:T(8,128)(2,1)S(1)}, f32[32,128]{1,0:T(8,128)S(1)}) custom-call(bf16[256,512]{1,0:T(8,128)(2,1)} %constant.2.clone.table_hbm, bf16[16,64,512]{2,1,0:T(8,128)(2,1)} %traces_hbm.1, s32[16,64]{1,0:T(8,128)} %valid_hbm.1, s32[1,64]{1,0:T(1,128)} %bitcast.1), custom_call_target="tpu_custom_call" | custom-call | tf_op jit(solution)/shard_map/exchange/pallas_call | solution.py:271
  30.5 1.5 %finish.1 = f32[32,64,256]{2,1,0:T(8,128)} custom-call(bf16[32,128,128]{2,1,0:T(8,128)(2,1)S(1)} %get-tuple-element.7.stack_ref, f32[32,128]{1,0:T(8,128)S(1)} %get-tuple-element.8.weight_ref), custom_call_target="tpu_custom_call" | custom-call | tf_op jit(solution)/shard_map/finish/pallas_call | solution.py:323

commit v5 on v4

--- a/solution.py
+++ b/solution.py
@@ -168,7 +168,7 @@
 
     shift = lax.rem(lax.broadcasted_iota(jnp.int32, (1, LANES), 1), width)
     band = BAND // groups
-    order = sorted({(step[0], step[2]) for step in steps}, key=lambda s: -hops((s[0], 0, s[1], 0)))
+    order = sorted(sorted({(step[0], step[2]) for step in steps}), key=lambda s: -hops((s[0], 0, s[1], 0)))
 
     def early(a):
         return max(0, (own - width * a - width) // band)
@@ -190,36 +190,30 @@
             by //= 2
         stack[b, a, band * start : band * stop] = product[: band * (stop - start)].astype(jnp.bfloat16)
 
-        def send_stack(d_hi, d_z):
-            to_win = win_at(d_hi, d_z)
-
-            def send():
-                pltpu.make_async_remote_copy(
-                    src_ref=stack.at[b, a, pl.ds(to_win * band, band)],
-                    dst_ref=landing.at[b * team + me],
-                    send_sem=send_out,
-                    recv_sem=recv_out.at[b],
-                    device_id={"chan": base + a, "win": to_win},
-                    device_id_type=MESH,
-                ).start()
-
-            if start == 0 and stop == groups:
-                send()
-            else:
-                pl.when((to_win >= start) & (to_win < stop))(send)
-
-        for d_hi, d_z in order[:-1]:
-            send_stack(d_hi, d_z)
-
-        @pl.when(lane_of != a)
+        def send_stack(to_win):
+            pltpu.make_async_remote_copy(
+                src_ref=stack.at[b, a, pl.ds(to_win * band, band)],
+                dst_ref=landing.at[b * team + me],
+                send_sem=send_out,
+                recv_sem=recv_out.at[b],
+                device_id={"chan": base + a, "win": to_win},
+                device_id_type=MESH,
+            ).start()
+
+        if stop - start <= width // band:
+            for to_win in range(start, stop):
+                pl.when((lane_of != a) | (win != to_win))(functools.partial(send_stack, to_win))
+        else:
+            for d_hi, d_z in order:
+                to_win = win_at(d_hi, d_z)
+                wanted = (to_win >= start) & (to_win < stop)
+                if (d_hi, d_z) == (0, 0):
+                    wanted = wanted & (lane_of != a)
+                pl.when(wanted)(functools.partial(send_stack, to_win))
+
+        @pl.when((lane_of == a) & (win >= start) & (win < stop))
         def _():
-            send_stack(0, 0)
-
-        if stop == groups:
-
-            @pl.when(lane_of == a)
-            def _():
-                landing[b * team + me] = stack[b, a, pl.ds(pl.multiple_of(win * band, band), band)]
+            landing[b * team + me] = stack[b, a, pl.ds(pl.multiple_of(win * band, band), band)]
 
     def multiply_early(b):
         for a in range(near):
@@ -227,10 +221,13 @@
                 piece(b, a, 0, early(a))
 
     def multiply(b):
-        for a in range(near):
-            halo = rows.at[b, pl.ds(own + width * a, width)]
-            pltpu.make_async_copy(halo, halo, recv_halo.at[b * near + a]).wait()
-            piece(b, a, early(a), groups)
+        step = width // band
+        for h in range(near):
+            halo = rows.at[b, pl.ds(own + width * h, width)]
+            pltpu.make_async_copy(halo, halo, recv_halo.at[b * near + h]).wait()
+            for a in range(near - 1, h - 1, -1):
+                start = step * (near - 1 - a + h)
+                piece(b, a, start, start + step)
 
     for b in range(bins):
         turn(b)

time: 32.1 us -> 31.7 us (0.988)
  the two profiles are of different devices: /device:TPU:27 before, /device:TPU:25 now
where the time goes in v5:
time: 31.7 us; the launch traced here: 31.6 us
  Pallas kernels  31.6 us (100%)
    pallas_call x1, Pallas kernels, exchange(): pl.pallas_call(functools.partial(exchange_kernel, groups, near, 1.0 / mat...  30 us
    pallas_call x1, Pallas kernels, finish(): pl.pallas_call(functools.partial(finish_kernel, parts), out_shape=jax.Sha...  1.51 us

profile of v5, /device:TPU:25, one launch (start us, length us, event | category | flops | bytes accessed | tf_op | source)
XLA Modules:
  0.0 31.6 jit_solution(4296709709449196319)
XLA Ops:
  0.0 30.0 %exchange.1 = (bf16[32,128,128]{2,1,0:T(8,128)(2,1)S(1)}, f32[32,128]{1,0:T(8,128)S(1)}) custom-call(bf16[256,512]{1,0:T(8,128)(2,1)} %constant.2.clone.table_hbm, bf16[16,64,512]{2,1,0:T(8,128)(2,1)} %traces_hbm.1, s32[16,64]{1,0:T(8,128)} %valid_hbm.1, s32[1,64]{1,0:T(1,128)} %bitcast.1), custom_call_target="tpu_custom_call" | custom-call | tf_op jit(solution)/shard_map/exchange/pallas_call | solution.py:268
  30.1 1.5 %finish.1 = f32[32,64,256]{2,1,0:T(8,128)} custom-call(bf16[32,128,128]{2,1,0:T(8,128)(2,1)S(1)} %get-tuple-element.7.stack_ref, f32[32,128]{1,0:T(8,128)S(1)} %get-tuple-element.8.weight_ref), custom_call_target="tpu_custom_call" | custom-call | tf_op jit(solution)/shard_map/finish/pallas_call | solution.py:320

commit v6 on v5

--- a/solution.py
+++ b/solution.py
@@ -190,6 +190,7 @@
             by //= 2
         stack[b, a, band * start : band * stop] = product[: band * (stop - start)].astype(jnp.bfloat16)
 
+    def dispatch(b, a, start, stop):
         def send_stack(to_win):
             pltpu.make_async_remote_copy(
                 src_ref=stack.at[b, a, pl.ds(to_win * band, band)],
@@ -215,25 +216,29 @@
         def _():
             landing[b * team + me] = stack[b, a, pl.ds(pl.multiple_of(win * band, band), band)]
 
+    def pieces(b, parts):
+        for part in parts:
+            piece(b, *part)
+        for part in parts:
+            dispatch(b, *part)
+
     def multiply_early(b):
-        for a in range(near):
-            if early(a):
-                piece(b, a, 0, early(a))
+        pieces(b, [(a, 0, early(a)) for a in range(near) if early(a)])
 
     def multiply(b):
         step = width // band
         for h in range(near):
             halo = rows.at[b, pl.ds(own + width * h, width)]
             pltpu.make_async_copy(halo, halo, recv_halo.at[b * near + h]).wait()
-            for a in range(near - 1, h - 1, -1):
-                start = step * (near - 1 - a + h)
-                piece(b, a, start, start + step)
+            starts = [(a, step * (near - 1 - a + h)) for a in range(near - 1, h - 1, -1)]
+            pieces(b, [(a, start, start + step) for a, start in starts])
 
     for b in range(bins):
         turn(b)
         multiply_early(b)
-        if b > 0:
-            multiply(b - 1)
+        if b > 1:
+            multiply(b - 2)
+    multiply(bins - 2)
     multiply(bins - 1)
 
     reach = jnp.concatenate([reach_ref[...], reach_ref[...]], axis=1)
@@ -314,7 +319,7 @@
 
 def finish(stacked, weights, width):
     band = stacked.shape[0]
-    parts = 8
+    parts = 4
     stacked = pltpu.with_memory_space_constraint(stacked, pltpu.VMEM)
     weights = pltpu.with_memory_space_constraint(weights, pltpu.VMEM)
     return pl.pallas_call(

time: 31.7 us -> 31.4 us (level)
  the two profiles are of different devices: /device:TPU:25 before, /device:TPU:27 now
where the time goes in v6:
time: 31.4 us; the launch traced here: 31.3 us
  Pallas kernels  31.3 us (100%)
    pallas_call x1, Pallas kernels, exchange(): pl.pallas_call(functools.partial(exchange_kernel, groups, near, 1.0 / mat...  29.7 us
    pallas_call x1, Pallas kernels, finish(): pl.pallas_call(functools.partial(finish_kernel, parts), out_shape=jax.Sha...  1.55 us

profile of v6, /device:TPU:27, one launch (start us, length us, event | category | flops | bytes accessed | tf_op | source)
XLA Modules:
  0.0 31.3 jit_solution(848795906367309057)
XLA Ops:
  0.0 29.7 %exchange.1 = (bf16[32,128,128]{2,1,0:T(8,128)(2,1)S(1)}, f32[32,128]{1,0:T(8,128)S(1)}) custom-call(bf16[256,512]{1,0:T(8,128)(2,1)} %constant.2.clone.table_hbm, bf16[16,64,512]{2,1,0:T(8,128)(2,1)} %traces_hbm.1, s32[16,64]{1,0:T(8,128)} %valid_hbm.1, s32[1,64]{1,0:T(1,128)} %bitcast.1), custom_call_target="tpu_custom_call" | custom-call | tf_op jit(solution)/shard_map/exchange/pallas_call | solution.py:273
  29.7 1.6 %finish.1 = f32[32,64,256]{2,1,0:T(8,128)} custom-call(bf16[32,128,128]{2,1,0:T(8,128)(2,1)S(1)} %get-tuple-element.7.stack_ref, f32[32,128]{1,0:T(8,128)S(1)} %get-tuple-element.8.weight_ref), custom_call_target="tpu_custom_call" | custom-call | tf_op jit(solution)/shard_map/finish/pallas_call | solution.py:325
